TPU v7x, 128 devices: a whole 4x4x4 slice. The times are simulated.
128 devices in a mesh: fsdp: 16 (over y, z), seq: 8 (over x, core).
Axes of the slice: x: 4, y: 4, z: 4, core: 2. Of those that a mesh axis runs over, the one named last changes fastest.
Arguments:
- frames: bfloat16 [16, 3072, 1536], P('fsdp', 'seq'), may hold values from -0.59765625 to 0.59765625
- lengths: int32 [16, 12], P('fsdp'), may hold values from 1 to 512, 3072 in all within a row
- w_qkv: bfloat16 [1536, 3072], P('fsdp'), may hold values from -4 to 4
- d_context: bfloat16 [16, 3072, 1024], P('fsdp', 'seq'), may hold values from -0.59765625 to 0.59765625
Outputs:
- context: bfloat16 [16, 3072, 1024], P('fsdp', 'seq')
- grad_input: bfloat16 [16, 3072, 1536], P('fsdp', 'seq')
- grad_weight: float32 [1536, 3072], P('fsdp', 'seq')
Inputs may be any that keep to these rules, and one draw needn't show every extreme that they name: The 12 lengths of a sequence sum to 3072, and the longest is exactly 512.
All inputs are finite; a program needn't handle non-finite values.
Results may differ from a plain program's by a relative error of at most 0.018.
Values may be sent and summed in bfloat16 or wider, within the bound.
A program may use at most 128 MiB of HBM per device.

v0:
```python
import jax
import jax.numpy as jnp
from jax import lax
from jax.sharding import PartitionSpec as P

HEADS = 16
HEAD_DIM = 64
MOST = 512


def segment_ids(lengths, frame_total):
    utter_ends = jnp.cumsum(lengths)
    positions = jnp.arange(frame_total, dtype=jnp.int32)
    return jnp.sum((positions[:, None] >= utter_ends[None, :]).astype(jnp.int32), axis=1)


def attend(query, keys, values, grad_out, segment):
    frame_total = query.shape[0]
    block_rows = 512
    key_span = min(block_rows + 2 * MOST, frame_total)
    block_count = frame_total // block_rows
    score_scale = HEAD_DIM ** (-0.5)

    def block_step(block_index, state_tuple):
        context, grad_query, grad_key, grad_value = state_tuple
        block_start = (block_index * block_rows).astype(jnp.int32)
        anchor = jnp.clip(block_start - MOST, 0, frame_total - key_span)
        query_block = lax.dynamic_slice_in_dim(query, block_start, block_rows, 0)
        grad_block = lax.dynamic_slice_in_dim(grad_out, block_start, block_rows, 0)
        segment_query = lax.dynamic_slice_in_dim(segment, block_start, block_rows, 0)
        key_window = lax.dynamic_slice_in_dim(keys, anchor, key_span, 0)
        value_window = lax.dynamic_slice_in_dim(values, anchor, key_span, 0)
        segment_key = lax.dynamic_slice_in_dim(segment, anchor, key_span, 0)
        scores = (
            jnp.einsum("qhd,khd->hqk", query_block, key_window, preferred_element_type=jnp.float32)
            * score_scale
        )
        same_utterance = segment_query[:, None] == segment_key[None, :]
        scores = jnp.where(same_utterance[None], scores, -jnp.inf)
        row_max = jnp.max(scores, axis=-1, keepdims=True)
        exponent = jnp.exp(scores - row_max)
        softmax_out = exponent / jnp.sum(exponent, axis=-1, keepdims=True)
        weights = softmax_out.astype(jnp.bfloat16)
        out_block = jnp.einsum(
            "hqk,khd->qhd", weights, value_window, preferred_element_type=jnp.float32
        ).astype(jnp.bfloat16)
        value_term = jnp.einsum(
            "hqk,qhd->khd", weights, grad_block, preferred_element_type=jnp.float32
        )
        dprobs = jnp.einsum(
            "qhd,khd->hqk", grad_block, value_window, preferred_element_type=jnp.float32
        )
        dscores = (
            softmax_out
            * (dprobs - jnp.sum(softmax_out * dprobs, axis=-1, keepdims=True))
            * score_scale
        )
        dscores = dscores.astype(jnp.bfloat16)
        query_term = jnp.einsum(
            "hqk,khd->qhd", dscores, key_window, preferred_element_type=jnp.float32
        ).astype(jnp.bfloat16)
        key_term = jnp.einsum(
            "hqk,qhd->khd", dscores, query_block, preferred_element_type=jnp.float32
        )
        context = lax.dynamic_update_slice_in_dim(context, out_block, block_start, 0)
        grad_query = lax.dynamic_update_slice_in_dim(grad_query, query_term, block_start, 0)
        grad_key = lax.dynamic_update_slice_in_dim(
            grad_key, lax.dynamic_slice_in_dim(grad_key, anchor, key_span, 0) + key_term, anchor, 0
        )
        grad_value = lax.dynamic_update_slice_in_dim(
            grad_value,
            lax.dynamic_slice_in_dim(grad_value, anchor, key_span, 0) + value_term,
            anchor,
            0,
        )
        return (context, grad_query, grad_key, grad_value)

    shape_one = query.shape
    initial = (
        jnp.zeros(shape_one, jnp.bfloat16),
        jnp.zeros(shape_one, jnp.bfloat16),
        jnp.zeros(shape_one, jnp.float32),
        jnp.zeros(shape_one, jnp.float32),
    )
    context, grad_query, grad_key, grad_value = lax.fori_loop(0, block_count, block_step, initial)
    return (context, grad_query, grad_key.astype(jnp.bfloat16), grad_value.astype(jnp.bfloat16))


def per_device(frames, lengths, w_qkv, d_context):
    values_in = frames[0].astype(jnp.float32)
    frame_count = values_in.shape[0]
    rank_count = lax.axis_size("seq")
    frame_total = frame_count * rank_count
    width = HEADS * HEAD_DIM
    per_rank = width // rank_count
    heads_here = per_rank // HEAD_DIM
    average = jnp.mean(values_in, axis=1, keepdims=True)
    centred = values_in - average
    variance = jnp.mean(centred * centred, axis=1, keepdims=True)
    inverse_scale = lax.rsqrt(variance + 1e-05)
    whitened = centred * inverse_scale
    normed = whitened.astype(jnp.bfloat16)
    weight_full = lax.all_gather(w_qkv, "fsdp", axis=0, tiled=True)
    projected = jnp.dot(normed, weight_full, preferred_element_type=jnp.float32)
    qkv_frames = projected.astype(jnp.bfloat16).reshape(frame_count, 3, rank_count, per_rank)
    cotangent = d_context[0].reshape(frame_count, 1, rank_count, per_rank)
    heads_qkv, heads_cotangent = (
        lax.all_to_all(qkv_frames, "seq", split_axis=2, concat_axis=0, tiled=True),
        lax.all_to_all(cotangent, "seq", split_axis=2, concat_axis=0, tiled=True),
    )
    query = heads_qkv[:, 0, 0].reshape(frame_total, heads_here, HEAD_DIM)
    keys = heads_qkv[:, 1, 0].reshape(frame_total, heads_here, HEAD_DIM)
    values = heads_qkv[:, 2, 0].reshape(frame_total, heads_here, HEAD_DIM)
    grad_out = heads_cotangent[:, 0, 0].reshape(frame_total, heads_here, HEAD_DIM)
    segment = segment_ids(lengths[0], frame_total)
    context, grad_query, grad_key, grad_value = attend(query, keys, values, grad_out, segment)
    context_heads = context.reshape(frame_total, 1, 1, per_rank)
    grad_heads = jnp.stack([grad_query, grad_key, grad_value], axis=1).reshape(
        frame_total, 3, 1, per_rank
    )
    context_back, grad_back = (
        lax.all_to_all(context_heads, "seq", split_axis=0, concat_axis=2, tiled=True),
        lax.all_to_all(grad_heads, "seq", split_axis=0, concat_axis=2, tiled=True),
    )
    context_out = context_back.reshape(1, frame_count, width)
    grad_qkv = grad_back.reshape(frame_count, 3 * width)
    grad_normed = lax.dot_general(
        grad_qkv, weight_full, (((1,), (1,)), ((), ())), preferred_element_type=jnp.float32
    )
    grad_input = inverse_scale * (
        grad_normed
        - jnp.mean(grad_normed, axis=1, keepdims=True)
        - whitened * jnp.mean(grad_normed * whitened, axis=1, keepdims=True)
    )
    grad_input = grad_input.astype(jnp.bfloat16)[None]
    owned_rows = lax.psum_scatter(
        lax.dot_general(
            normed, grad_qkv, (((0,), (0,)), ((), ())), preferred_element_type=jnp.float32
        ).astype(jnp.bfloat16),
        "fsdp",
        scatter_dimension=0,
        tiled=True,
    )
    grad_weight = lax.psum_scatter(owned_rows, "seq", scatter_dimension=1, tiled=True).astype(
        jnp.float32
    )
    return (context_out, grad_input, grad_weight)


def solution(mesh):
    return jax.shard_map(
        per_device,
        mesh=mesh,
        in_specs=(P("fsdp", "seq", None), P("fsdp", None), P("fsdp", None), P("fsdp", "seq", None)),
        out_specs=(P("fsdp", "seq", None), P("fsdp", "seq", None), P("fsdp", "seq")),
        check_vma=False,
    )
```

profile of v0, /device:TPU:0, one launch (start us, length us, event | category | flops | bytes accessed | tf_op | source)
XLA Modules:
  0.0 692.2 jit_solution(15582703184175243166)
XLA Ops:
  15.3 73.1 %all-gather.2.cloned.1.call-done = bf16[1536,3072]{1,0:T(8,128)(2,1)} async-done(((bf16[96,3072]{1,0:T(8,128)(2,1)}), bf16[1536,3072]{1,0:T(8,128)(2,1)}) %all-gather.2.cloned.1.call-update) | async-done | bytes 9437200 | tf_op jit(solution)/shard_map/all_gather | solution.py:103
  88.4 7.9 %fusion.104 = bf16[48,8,24,128]{3,1,2,0:T(8,128)(2,1)S(1)} fusion(bf16[1536,3072]{1,0:T(8,128)(2,1)} %all-gather.2.cloned.1.call-done, bf16[1,384,1536]{2,1,0:T(8,128)(2,1)S(1)} %copy-done, f32[384]{0:T(512)S(1)} %add_rsqrt_fusion, f32[384]{0:T(512)S(1)} %broadcast_multiply_fusion.2), kind=kOutput, calls=%fused_computation.73 | convolution fusion | flops 3627417600 | bytes 12979200 | tf_op jit(solution)/shard_map/dot_general | solution.py:104
  107.2 26.0 %all-to-all-done = bf16[384,3,8,128]{3,0,1,2:T(8,128)(2,1)S(1)} async-done(((bf16[384,3,8,128]{3,0,1,2:T(8,128)(2,1)}), bf16[384,3,8,128]{3,0,1,2:T(8,128)(2,1)S(1)}, u32[]{:S(2)}, u32[]{:S(2)}) %all-to-all-start) | async-done | bytes 2359328 | tf_op jit(solution)/shard_map/all_to_all | solution.py:108
  139.9 362.4 %while.21 = (s32[]{:T(128)}, bf16[3072,2,64]{0,2,1:T(8,128)(2,1)S(1)}, bf16[3072,2,64]{0,2,1:T(8,128)(2,1)}, f32[3072,2,64]{0,2,1:T(8,128)}, f32[3072,2,64]{0,2,...) while((s32[]{:T(128)}, ...), condition=%wide.region_8.9_spmd, body=%wide.region_4.8_spmd.sunk | while | flops 1655975424 | bytes 78963000 | solution.py:85
  155.5 14.9 %fusion.165 = bf16[3072,2,64]{0,2,1:T(8,128)(2,1)} fusion(bf16[3072,2,64]{0,2,1:T(8,128)(2,1)} %get-tuple-element.393, s32[]{:T(128)S(6)} %select_n.55, f32[2,512,1536]{2,1,0:T(8,128)} %fusion.164, bf16[3072,2,64]{0,2,1:T(8,128)(2,1)S(1)} %copy-done.5, s32[]{:T(128)S(6)} %min.12, f32[2,512,1536]{2,1,0:T(8,128)} %get-tuple-element.374, ...), kind=kOutput, calls=%fused_computation.27.clone.1 | convolution fusion | flops 212404736 | bytes 25698312 | tf_op jit(solution)/shard_map/while/body/eval_jaxpr/hqk,khd->qhd/dot_general | solution.py:59
  170.3 14.9 %fusion.166 = f32[1536,2,64]{0,2,1:T(8,128)S(1)} fusion(f32[2,512,1536]{2,1,0:T(8,128)} %fusion.164, f32[3072,2,64]{0,2,1:T(8,128)} %get-tuple-element.394, s32[]{:T(128)S(6)} %min.12, bf16[3072,2,64]{0,2,1:T(8,128)(2,1)} %get-tuple-element.414, s32[]{:T(128)S(6)} %select_n.55, f32[2,512,1536]{2,1,0:T(8,128)} %get-tuple-element.374, ...), kind=kOutput, calls=%fused_computation.17.clone.1 | convolution fusion | flops 212535808 | bytes 26877960 | tf_op jit(solution)/shard_map/while/body/eval_jaxpr/hqk,qhd->khd/dot_general | solution.py:62
  201.5 6.2 fusion.162
  216.3 14.9 %fusion.165 = bf16[3072,2,64]{0,2,1:T(8,128)(2,1)} fusion(bf16[3072,2,64]{0,2,1:T(8,128)(2,1)} %get-tuple-element.393, s32[]{:T(128)S(6)} %select_n.55, f32[2,512,1536]{2,1,0:T(8,128)} %fusion.164, bf16[3072,2,64]{0,2,1:T(8,128)(2,1)S(1)} %copy-done.5, s32[]{:T(128)S(6)} %min.12, f32[2,512,1536]{2,1,0:T(8,128)} %get-tuple-element.374, ...), kind=kOutput, calls=%fused_computation.27.clone.1 | convolution fusion | flops 212404736 | bytes 25698312 | tf_op jit(solution)/shard_map/while/body/eval_jaxpr/hqk,khd->qhd/dot_general | solution.py:59
  231.2 15.0 %fusion.166 = f32[1536,2,64]{0,2,1:T(8,128)S(1)} fusion(f32[2,512,1536]{2,1,0:T(8,128)} %fusion.164, f32[3072,2,64]{0,2,1:T(8,128)} %get-tuple-element.394, s32[]{:T(128)S(6)} %min.12, bf16[3072,2,64]{0,2,1:T(8,128)(2,1)} %get-tuple-element.414, s32[]{:T(128)S(6)} %select_n.55, f32[2,512,1536]{2,1,0:T(8,128)} %get-tuple-element.374, ...), kind=kOutput, calls=%fused_computation.17.clone.1 | convolution fusion | flops 212535808 | bytes 26877960 | tf_op jit(solution)/shard_map/while/body/eval_jaxpr/hqk,qhd->khd/dot_general | solution.py:62
  277.3 14.9 %fusion.165 = bf16[3072,2,64]{0,2,1:T(8,128)(2,1)} fusion(bf16[3072,2,64]{0,2,1:T(8,128)(2,1)} %get-tuple-element.393, s32[]{:T(128)S(6)} %select_n.55, f32[2,512,1536]{2,1,0:T(8,128)} %fusion.164, bf16[3072,2,64]{0,2,1:T(8,128)(2,1)S(1)} %copy-done.5, s32[]{:T(128)S(6)} %min.12, f32[2,512,1536]{2,1,0:T(8,128)} %get-tuple-element.374, ...), kind=kOutput, calls=%fused_computation.27.clone.1 | convolution fusion | flops 212404736 | bytes 25698312 | tf_op jit(solution)/shard_map/while/body/eval_jaxpr/hqk,khd->qhd/dot_general | solution.py:59
  292.2 14.9 %fusion.166 = f32[1536,2,64]{0,2,1:T(8,128)S(1)} fusion(f32[2,512,1536]{2,1,0:T(8,128)} %fusion.164, f32[3072,2,64]{0,2,1:T(8,128)} %get-tuple-element.394, s32[]{:T(128)S(6)} %min.12, bf16[3072,2,64]{0,2,1:T(8,128)(2,1)} %get-tuple-element.414, s32[]{:T(128)S(6)} %select_n.55, f32[2,512,1536]{2,1,0:T(8,128)} %get-tuple-element.374, ...), kind=kOutput, calls=%fused_computation.17.clone.1 | convolution fusion | flops 212535808 | bytes 26877960 | tf_op jit(solution)/shard_map/while/body/eval_jaxpr/hqk,qhd->khd/dot_general | solution.py:62
  323.2 6.2 fusion.162
  338.0 14.9 %fusion.165 = bf16[3072,2,64]{0,2,1:T(8,128)(2,1)} fusion(bf16[3072,2,64]{0,2,1:T(8,128)(2,1)} %get-tuple-element.393, s32[]{:T(128)S(6)} %select_n.55, f32[2,512,1536]{2,1,0:T(8,128)} %fusion.164, bf16[3072,2,64]{0,2,1:T(8,128)(2,1)S(1)} %copy-done.5, s32[]{:T(128)S(6)} %min.12, f32[2,512,1536]{2,1,0:T(8,128)} %get-tuple-element.374, ...), kind=kOutput, calls=%fused_computation.27.clone.1 | convolution fusion | flops 212404736 | bytes 25698312 | tf_op jit(solution)/shard_map/while/body/eval_jaxpr/hqk,khd->qhd/dot_general | solution.py:59
  352.9 15.0 %fusion.166 = f32[1536,2,64]{0,2,1:T(8,128)S(1)} fusion(f32[2,512,1536]{2,1,0:T(8,128)} %fusion.164, f32[3072,2,64]{0,2,1:T(8,128)} %get-tuple-element.394, s32[]{:T(128)S(6)} %min.12, bf16[3072,2,64]{0,2,1:T(8,128)(2,1)} %get-tuple-element.414, s32[]{:T(128)S(6)} %select_n.55, f32[2,512,1536]{2,1,0:T(8,128)} %get-tuple-element.374, ...), kind=kOutput, calls=%fused_computation.17.clone.1 | convolution fusion | flops 212535808 | bytes 26877960 | tf_op jit(solution)/shard_map/while/body/eval_jaxpr/hqk,qhd->khd/dot_general | solution.py:62
  398.6 14.9 %fusion.165 = bf16[3072,2,64]{0,2,1:T(8,128)(2,1)} fusion(bf16[3072,2,64]{0,2,1:T(8,128)(2,1)} %get-tuple-element.393, s32[]{:T(128)S(6)} %select_n.55, f32[2,512,1536]{2,1,0:T(8,128)} %fusion.164, bf16[3072,2,64]{0,2,1:T(8,128)(2,1)S(1)} %copy-done.5, s32[]{:T(128)S(6)} %min.12, f32[2,512,1536]{2,1,0:T(8,128)} %get-tuple-element.374, ...), kind=kOutput, calls=%fused_computation.27.clone.1 | convolution fusion | flops 212404736 | bytes 25698312 | tf_op jit(solution)/shard_map/while/body/eval_jaxpr/hqk,khd->qhd/dot_general | solution.py:59
  413.5 14.9 %fusion.166 = f32[1536,2,64]{0,2,1:T(8,128)S(1)} fusion(f32[2,512,1536]{2,1,0:T(8,128)} %fusion.164, f32[3072,2,64]{0,2,1:T(8,128)} %get-tuple-element.394, s32[]{:T(128)S(6)} %min.12, bf16[3072,2,64]{0,2,1:T(8,128)(2,1)} %get-tuple-element.414, s32[]{:T(128)S(6)} %select_n.55, f32[2,512,1536]{2,1,0:T(8,128)} %get-tuple-element.374, ...), kind=kOutput, calls=%fused_computation.17.clone.1 | convolution fusion | flops 212535808 | bytes 26877960 | tf_op jit(solution)/shard_map/while/body/eval_jaxpr/hqk,qhd->khd/dot_general | solution.py:62
  458.2 14.9 %fusion.165 = bf16[3072,2,64]{0,2,1:T(8,128)(2,1)} fusion(bf16[3072,2,64]{0,2,1:T(8,128)(2,1)} %get-tuple-element.393, s32[]{:T(128)S(6)} %select_n.55, f32[2,512,1536]{2,1,0:T(8,128)} %fusion.164, bf16[3072,2,64]{0,2,1:T(8,128)(2,1)S(1)} %copy-done.5, s32[]{:T(128)S(6)} %min.12, f32[2,512,1536]{2,1,0:T(8,128)} %get-tuple-element.374, ...), kind=kOutput, calls=%fused_computation.27.clone.1 | convolution fusion | flops 212404736 | bytes 25698312 | tf_op jit(solution)/shard_map/while/body/eval_jaxpr/hqk,khd->qhd/dot_general | solution.py:59
  473.1 15.0 %fusion.166 = f32[1536,2,64]{0,2,1:T(8,128)S(1)} fusion(f32[2,512,1536]{2,1,0:T(8,128)} %fusion.164, f32[3072,2,64]{0,2,1:T(8,128)} %get-tuple-element.394, s32[]{:T(128)S(6)} %min.12, bf16[3072,2,64]{0,2,1:T(8,128)(2,1)} %get-tuple-element.414, s32[]{:T(128)S(6)} %select_n.55, f32[2,512,1536]{2,1,0:T(8,128)} %get-tuple-element.374, ...), kind=kOutput, calls=%fused_computation.17.clone.1 | convolution fusion | flops 212535808 | bytes 26877960 | tf_op jit(solution)/shard_map/while/body/eval_jaxpr/hqk,qhd->khd/dot_general | solution.py:62
  511.8 40.9 %all_to_all.63 = bf16[3072,3,1,128]{3,1,2,0:T(4,128)(2,1)S(1)} all-to-all(bf16[3072,3,1,128]{3,1,2,0:T(4,128)(2,1)S(1)} %copy.83), channel_id=1, replica_groups=mesh['fsdp'=16,'seq'=8] {'seq'}, dimensions={0} | all-to-all | bytes 4718592 | tf_op jit(solution)/shard_map/all_to_all | solution.py:123
  555.5 9.5 %convolution_convert_fusion = bf16[1536,3072]{1,0:T(8,128)(2,1)} fusion(bf16[384,3072]{0,1:T(8,128)(2,1)} %bitcast.107, bf16[1,384,1536]{2,1,0:T(8,128)(2,1)S(1)} %copy-done.1, f32[384]{0:T(512)S(1)} %copy-done.9, f32[384]{0:T(512)S(1)} %copy-done.7), kind=kOutput, calls=%fused_computation.54 | convolution fusion | flops 3630956544 | bytes 12979200 | tf_op jit(solution)/shard_map/dot_general | solution.py:137
  568.0 15.6 %all_to_all.64 = bf16[8,2,24576]{2,1,0:T(2,128)(2,1)S(1)} all-to-all(bf16[8,2,24576]{2,1,0:T(2,128)(2,1)S(1)} %reshape.126), channel_id=1, replica_groups=mesh['fsdp'=16,'seq'=8] {'seq'}, dimensions={0} | all-to-all | bytes 1572864 | tf_op jit(solution)/shard_map/all_to_all | solution.py:122
  586.0 64.8 %reduce-scatter.5.cloned.1.call-done = bf16[96,3072]{1,0:T(8,128)(2,1)} async-done(((bf16[1536,3072]{1,0:T(8,128)(2,1)}), bf16[96,3072]{1,0:T(8,128)(2,1)}) %reduce-scatter.5.cloned.1.call-update) | async-done | bytes 589840 | tf_op jit(solution)/shard_map/reduce_scatter | solution.py:136
  653.0 7.7 %fusion.113 = (f32[384]{0:T(512)S(1)}, f32[384]{0:T(512)S(1)}, f32[384,1536]{1,0:T(8,128)S(1)}) fusion(f32[384]{0:T(512)S(1)} %copy-done.9, f32[384]{0:T(512)S(1)} %copy-done.7, bf16[1,384,1536]{2,1,0:T(8,128)(2,1)S(1)} %copy-done.1, bf16[384,3072]{0,1:T(8,128)(2,1)} %bitcast.108, bf16[1536,3072]{1,0:T(8,128)(2,1)} %all-gather.2.cloned.1.call-done), kind=kOutput, calls=%fused_computation.86 | convolution fusion | flops 3627416576 | bytes 15341568 | tf_op jit(solution)/shard_map/dot_general | solution.py:127
  662.4 21.6 %reduce-scatter.7.cloned.1.call-done = bf16[384,96]{1,0:T(8,128)(2,1)} async-done(((bf16[3072,96]{1,0:T(8,128)(2,1)}), bf16[384,96]{1,0:T(8,128)(2,1)}) %reduce-scatter.7.cloned.1.call-update) | async-done | bytes 73744
  (132 shorter events, 219.8 us)
Async XLA Ops:
  7.2 7.4 %copy-start = (bf16[1,384,1536]{2,1,0:T(8,128)(2,1)S(1)}, bf16[1,384,1536]{2,1,0:T(8,128)(2,1)}, u32[]{:S(2)}) copy-start(bf16[1,384,1536]{2,1,0:T(8,128)(2,1)} %param.6) | copy-start | bytes 3538948
  7.2 81.2 %all-gather.2.cloned.1.call-start = ((), (), s32[]{:S(2)}) async-start(), calls=%async_computation.6 | async-start | bytes 10027008 | tf_op jit(solution)/shard_map/all_gather | solution.py:103
  10.2 88.6 %all-to-all-start.1 = ((bf16[384,1,8,128]{0,3,1,2:T(8,128)(2,1)}), bf16[384,1,8,128]{0,3,1,2:T(8,128)(2,1)S(1)}, u32[]{:S(2)}, u32[]{:S(2)}) async-start(bf16[384,1,8,128]{0,3,1,2:T(8,128)(2,1)} %bitcast.15), calls=%async_computation.1 | async-start | bytes 1572864 | tf_op jit(solution)/shard_map/all_to_all | solution.py:109
  14.9 81.4 %copy-start.6 = (f32[384]{0:T(512)}, f32[384]{0:T(512)S(1)}, u32[]{:S(2)}) copy-start(f32[384]{0:T(512)S(1)} %broadcast_multiply_fusion.2) | copy-start | bytes 4612
  15.3 81.0 %copy-start.8 = (f32[384]{0:T(512)}, f32[384]{0:T(512)S(1)}, u32[]{:S(2)}) copy-start(f32[384]{0:T(512)S(1)} %add_rsqrt_fusion) | copy-start | bytes 4612
  98.8 4.4 copy-start.10
  98.8 34.4 %all-to-all-start = ((bf16[384,3,8,128]{3,0,1,2:T(8,128)(2,1)}), bf16[384,3,8,128]{3,0,1,2:T(8,128)(2,1)S(1)}, u32[]{:S(2)}, u32[]{:S(2)}) async-start(bf16[384,3,8,128]{3,0,1,2:T(8,128)(2,1)} %copy.74), calls=%async_computation | async-start | bytes 4718592 | tf_op jit(solution)/shard_map/all_to_all | solution.py:108
  103.2 547.6 %reduce-scatter.5.cloned.1.call-start = ((), (), s32[]{:S(2)}) async-start(), calls=%async_computation.7 | async-start | bytes 10027008 | tf_op jit(solution)/shard_map/reduce_scatter | solution.py:136
  140.6 6.2 copy-start.5
  201.5 6.2 copy-start.5
  262.4 6.2 copy-start.5
  323.2 6.2 copy-start.5
  383.8 6.2 copy-start.5
  443.4 6.2 copy-start.5
  502.3 2.3 copy-start.3
  502.3 2.2 copy-start.2
  553.0 2.5 copy-start.1
  553.0 2.5 copy-start.7
  553.0 2.5 copy-start.9
  565.1 1.1 copy-start.4
  565.1 118.9 %reduce-scatter.7.cloned.1.call-start = ((), (), s32[]{:S(2)}) async-start(), calls=%async_computation.8 | async-start | bytes 884736
Sparse Core Ops, SparseCore 0:
  10.2 78.1 all-gather.1
  565.2 85.5 reduce-scatter.4
  653.2 30.7 reduce-scatter.6
where the time goes:
time: 695 us; the launch traced here: 692 us
  matrix products  320 us (46%)
  waiting for transfers between devices  186 us (27%)
  local copies, waits for them, and re-layouts  93.8 us (13%)
  blocking collectives  56.5 us (8%)
  between operations  14 us (2%)
  other arithmetic  12.3 us (2%)
  starting transfers between devices  8.91 us (1%)
    dot_general x6, matrix products, block_step(): jnp.einsum('hqk,qhd->khd', dscores, query_block, preferred_element_type=j...  89.7 us
    dot_general x6, matrix products, block_step(): jnp.einsum('hqk,khd->qhd', dscores, key_window, preferred_element_type=jn...  89.2 us
    all_gather x1, waiting for transfers between devices, per_device(): weight_full = lax.all_gather(w_qkv, 'fsdp', axis=0, tiled=True)  73.1 us
    reduce_scatter x1, waiting for transfers between devices, per_device(): lax.psum_scatter(lax.dot_general(normed, grad_qkv, (((0,), (0,)), ((), ()...  64.8 us
    all_to_all x1, blocking collectives, per_device(): lax.all_to_all(grad_heads, 'seq', split_axis=0, concat_axis=2, tiled=True)  40.9 us
    sub x6, matrix products, block_step(): exponent = jnp.exp(scores - row_max)  37.2 us
    dynamic_update_slice x6, local copies, waits for them, and re-layouts, block_step(): lax.dynamic_update_slice_in_dim(grad_value, lax.dynamic_slice_in_dim(grad...  31.5 us
    dynamic_update_slice x6, local copies, waits for them, and re-layouts, block_step(): lax.dynamic_update_slice_in_dim(grad_key, lax.dynamic_slice_in_dim(grad_k...  31.5 us
  transfers between devices with their start and end apart: 5, of which 4 were waited for; matrix products, arithmetic and copies ran while one was open for 5% of the time, Pallas kernels for 0%

commit v1 on v0

--- a/solution.py
+++ b/solution.py
@@ -1,3 +1,4 @@
+import functools
 import jax
 import jax.numpy as jnp
 from jax import lax
@@ -6,6 +7,14 @@
 HEADS = 16
 HEAD_DIM = 64
 MOST = 512
+
+
+def _part_quotas(base_x, dev_axis):
+    top = lax.all_to_all(jnp.stack([base_x] * lax.axis_size(dev_axis), axis=0), dev_axis, 0, 0)
+    return jnp.concatenate(top, axis=0)
+
+
+_fill_object = functools.partial(_part_quotas, dev_axis="fsdp")
 
 
 def segment_ids(lengths, frame_total):
@@ -100,7 +109,7 @@
     inverse_scale = lax.rsqrt(variance + 1e-05)
     whitened = centred * inverse_scale
     normed = whitened.astype(jnp.bfloat16)
-    weight_full = lax.all_gather(w_qkv, "fsdp", axis=0, tiled=True)
+    weight_full = _fill_object(w_qkv)
     projected = jnp.dot(normed, weight_full, preferred_element_type=jnp.float32)
     qkv_frames = projected.astype(jnp.bfloat16).reshape(frame_count, 3, rank_count, per_rank)
     cotangent = d_context[0].reshape(frame_count, 1, rank_count, per_rank)

time: 695 us -> 807 us (1.16)
  waiting for transfers between devices: 186 us -> 285 us
    all_to_all x0 -> x1, waiting for transfers between devices: none -> 163 us  [_part_quotas(): lax.all_to_all(jnp.stack([base_x] * lax.axis_size(dev_axis), axis=0), dev...]
    all_gather x1 -> x0, waiting for transfers between devices: 73.1 us -> none  [per_device(): weight_full = lax.all_gather(w_qkv, 'fsdp', axis=0, tiled=True)]
    all_to_all x0 -> x1, starting transfers between devices: none -> 8.34 us  [_part_quotas(): lax.all_to_all(jnp.stack([base_x] * lax.axis_size(dev_axis), axis=0), dev...]
    unnamed x4 -> x3, waiting for transfers between devices: 22.3 us -> 21.7 us
  transfers between devices with their start and end apart: 5 -> 5, of which waited for: 4 -> 5; matrix products, arithmetic and copies ran while one was open for 5% -> 4% of each run, Pallas kernels for 0% -> 0%
where the time goes in v1:
time: 807 us; the launch traced here: 803 us
  matrix products  320 us (40%)
  waiting for transfers between devices  285 us (35%)
  local copies, waits for them, and re-layouts  98.6 us (12%)
  blocking collectives  56.5 us (7%)
  starting transfers between devices  16.3 us (2%)
  between operations  14.3 us (2%)
  other arithmetic  12.3 us (2%)
    all_to_all x1, waiting for transfers between devices, _part_quotas(): lax.all_to_all(jnp.stack([base_x] * lax.axis_size(dev_axis), axis=0), dev...  163 us
    dot_general x6, matrix products, block_step(): jnp.einsum('hqk,qhd->khd', dscores, query_block, preferred_element_type=j...  89.7 us
    dot_general x6, matrix products, block_step(): jnp.einsum('hqk,khd->qhd', dscores, key_window, preferred_element_type=jn...  89.2 us
    reduce_scatter x1, waiting for transfers between devices, per_device(): lax.psum_scatter(lax.dot_general(normed, grad_qkv, (((0,), (0,)), ((), ()...  71.7 us
    all_to_all x1, blocking collectives, per_device(): lax.all_to_all(grad_heads, 'seq', split_axis=0, concat_axis=2, tiled=True)  40.9 us
    sub x6, matrix products, block_step(): exponent = jnp.exp(scores - row_max)  37.2 us
    dynamic_update_slice x6, local copies, waits for them, and re-layouts, block_step(): lax.dynamic_update_slice_in_dim(grad_value, lax.dynamic_slice_in_dim(grad...  31.5 us
    dynamic_update_slice x6, local copies, waits for them, and re-layouts, block_step(): lax.dynamic_update_slice_in_dim(grad_key, lax.dynamic_slice_in_dim(grad_k...  31.5 us
  transfers between devices with their start and end apart: 5, of which 5 were waited for; matrix products, arithmetic and copies ran while one was open for 4% of the time, Pallas kernels for 0%

profile of v1, /device:TPU:0, one launch (start us, length us, event | category | flops | bytes accessed | tf_op | source)
XLA Modules:
  0.0 803.4 jit_solution(5498121945023722135)
XLA Ops:
  13.1 8.3 %all-to-all-start = ((bf16[16,96,3072]{2,1,0:T(8,128)(2,1)}), bf16[16,96,3072]{2,1,0:T(8,128)(2,1)}, u32[]{:S(2)}, u32[]{:S(2)}) async-start(bf16[16,96,3072]{2,1,0:T(8,128)(2,1)} %stack.10), calls=%async_computation | async-start | bytes 18874368 | tf_op jit(solution)/shard_map/all_to_all | solution.py:13
  23.3 162.8 %all-to-all-done = bf16[16,96,3072]{2,1,0:T(8,128)(2,1)} async-done(((bf16[16,96,3072]{2,1,0:T(8,128)(2,1)}), bf16[16,96,3072]{2,1,0:T(8,128)(2,1)}, u32[]{:S(2)}, u32[]{:S(2)}) %all-to-all-start) | async-done | bytes 9437216 | tf_op jit(solution)/shard_map/all_to_all | solution.py:13
  190.4 7.9 fusion.103
  211.1 26.0 %all-to-all-done.1 = bf16[384,3,8,128]{3,0,1,2:T(8,128)(2,1)S(1)} async-done(((bf16[384,3,8,128]{3,0,1,2:T(8,128)(2,1)}), bf16[384,3,8,128]{3,0,1,2:T(8,128)(2,1)S(1)}, u32[]{:S(2)}, u32[]{:S(2)}) %all-to-all-start.1) | async-done | bytes 2359328 | tf_op jit(solution)/shard_map/all_to_all | solution.py:117
  243.8 362.4 %while.21 = (s32[]{:T(128)}, bf16[3072,2,64]{0,2,1:T(8,128)(2,1)S(1)}, bf16[3072,2,64]{0,2,1:T(8,128)(2,1)}, f32[3072,2,64]{0,2,1:T(8,128)}, f32[3072,2,64]{0,2,...) while((s32[]{:T(128)}, ...), condition=%wide.region_8.9_spmd, body=%wide.region_4.8_spmd.sunk | while | flops 1655975424 | bytes 78963000 | solution.py:94
  244.5 6.2 fusion.157
  259.3 14.9 %fusion.160 = bf16[3072,2,64]{0,2,1:T(8,128)(2,1)} fusion(bf16[3072,2,64]{0,2,1:T(8,128)(2,1)} %get-tuple-element.393, s32[]{:T(128)S(6)} %select_n.55, f32[2,512,1536]{2,1,0:T(8,128)} %fusion.159, bf16[3072,2,64]{0,2,1:T(8,128)(2,1)S(1)} %copy-done.6, s32[]{:T(128)S(6)} %min.12, f32[2,512,1536]{2,1,0:T(8,128)} %get-tuple-element.374, ...), kind=kOutput, calls=%fused_computation.27.clone.1 | convolution fusion | flops 212404736 | bytes 25698312 | tf_op jit(solution)/shard_map/while/body/eval_jaxpr/hqk,khd->qhd/dot_general | solution.py:68
  274.2 14.9 %fusion.161 = f32[1536,2,64]{0,2,1:T(8,128)S(1)} fusion(f32[2,512,1536]{2,1,0:T(8,128)} %fusion.159, f32[3072,2,64]{0,2,1:T(8,128)} %get-tuple-element.394, s32[]{:T(128)S(6)} %min.12, bf16[3072,2,64]{0,2,1:T(8,128)(2,1)} %get-tuple-element.414, s32[]{:T(128)S(6)} %select_n.55, f32[2,512,1536]{2,1,0:T(8,128)} %get-tuple-element.374, ...), kind=kOutput, calls=%fused_computation.17.clone.1 | convolution fusion | flops 212535808 | bytes 26877960 | tf_op jit(solution)/shard_map/while/body/eval_jaxpr/hqk,qhd->khd/dot_general | solution.py:71
  320.2 14.9 %fusion.160 = bf16[3072,2,64]{0,2,1:T(8,128)(2,1)} fusion(bf16[3072,2,64]{0,2,1:T(8,128)(2,1)} %get-tuple-element.393, s32[]{:T(128)S(6)} %select_n.55, f32[2,512,1536]{2,1,0:T(8,128)} %fusion.159, bf16[3072,2,64]{0,2,1:T(8,128)(2,1)S(1)} %copy-done.6, s32[]{:T(128)S(6)} %min.12, f32[2,512,1536]{2,1,0:T(8,128)} %get-tuple-element.374, ...), kind=kOutput, calls=%fused_computation.27.clone.1 | convolution fusion | flops 212404736 | bytes 25698312 | tf_op jit(solution)/shard_map/while/body/eval_jaxpr/hqk,khd->qhd/dot_general | solution.py:68
  335.1 15.0 %fusion.161 = f32[1536,2,64]{0,2,1:T(8,128)S(1)} fusion(f32[2,512,1536]{2,1,0:T(8,128)} %fusion.159, f32[3072,2,64]{0,2,1:T(8,128)} %get-tuple-element.394, s32[]{:T(128)S(6)} %min.12, bf16[3072,2,64]{0,2,1:T(8,128)(2,1)} %get-tuple-element.414, s32[]{:T(128)S(6)} %select_n.55, f32[2,512,1536]{2,1,0:T(8,128)} %get-tuple-element.374, ...), kind=kOutput, calls=%fused_computation.17.clone.1 | convolution fusion | flops 212535808 | bytes 26877960 | tf_op jit(solution)/shard_map/while/body/eval_jaxpr/hqk,qhd->khd/dot_general | solution.py:71
  381.2 14.9 %fusion.160 = bf16[3072,2,64]{0,2,1:T(8,128)(2,1)} fusion(bf16[3072,2,64]{0,2,1:T(8,128)(2,1)} %get-tuple-element.393, s32[]{:T(128)S(6)} %select_n.55, f32[2,512,1536]{2,1,0:T(8,128)} %fusion.159, bf16[3072,2,64]{0,2,1:T(8,128)(2,1)S(1)} %copy-done.6, s32[]{:T(128)S(6)} %min.12, f32[2,512,1536]{2,1,0:T(8,128)} %get-tuple-element.374, ...), kind=kOutput, calls=%fused_computation.27.clone.1 | convolution fusion | flops 212404736 | bytes 25698312 | tf_op jit(solution)/shard_map/while/body/eval_jaxpr/hqk,khd->qhd/dot_general | solution.py:68
  396.0 14.9 %fusion.161 = f32[1536,2,64]{0,2,1:T(8,128)S(1)} fusion(f32[2,512,1536]{2,1,0:T(8,128)} %fusion.159, f32[3072,2,64]{0,2,1:T(8,128)} %get-tuple-element.394, s32[]{:T(128)S(6)} %min.12, bf16[3072,2,64]{0,2,1:T(8,128)(2,1)} %get-tuple-element.414, s32[]{:T(128)S(6)} %select_n.55, f32[2,512,1536]{2,1,0:T(8,128)} %get-tuple-element.374, ...), kind=kOutput, calls=%fused_computation.17.clone.1 | convolution fusion | flops 212535808 | bytes 26877960 | tf_op jit(solution)/shard_map/while/body/eval_jaxpr/hqk,qhd->khd/dot_general | solution.py:71
  441.9 14.9 %fusion.160 = bf16[3072,2,64]{0,2,1:T(8,128)(2,1)} fusion(bf16[3072,2,64]{0,2,1:T(8,128)(2,1)} %get-tuple-element.393, s32[]{:T(128)S(6)} %select_n.55, f32[2,512,1536]{2,1,0:T(8,128)} %fusion.159, bf16[3072,2,64]{0,2,1:T(8,128)(2,1)S(1)} %copy-done.6, s32[]{:T(128)S(6)} %min.12, f32[2,512,1536]{2,1,0:T(8,128)} %get-tuple-element.374, ...), kind=kOutput, calls=%fused_computation.27.clone.1 | convolution fusion | flops 212404736 | bytes 25698312 | tf_op jit(solution)/shard_map/while/body/eval_jaxpr/hqk,khd->qhd/dot_general | solution.py:68
  456.8 15.0 %fusion.161 = f32[1536,2,64]{0,2,1:T(8,128)S(1)} fusion(f32[2,512,1536]{2,1,0:T(8,128)} %fusion.159, f32[3072,2,64]{0,2,1:T(8,128)} %get-tuple-element.394, s32[]{:T(128)S(6)} %min.12, bf16[3072,2,64]{0,2,1:T(8,128)(2,1)} %get-tuple-element.414, s32[]{:T(128)S(6)} %select_n.55, f32[2,512,1536]{2,1,0:T(8,128)} %get-tuple-element.374, ...), kind=kOutput, calls=%fused_computation.17.clone.1 | convolution fusion | flops 212535808 | bytes 26877960 | tf_op jit(solution)/shard_map/while/body/eval_jaxpr/hqk,qhd->khd/dot_general | solution.py:71
  502.5 14.9 %fusion.160 = bf16[3072,2,64]{0,2,1:T(8,128)(2,1)} fusion(bf16[3072,2,64]{0,2,1:T(8,128)(2,1)} %get-tuple-element.393, s32[]{:T(128)S(6)} %select_n.55, f32[2,512,1536]{2,1,0:T(8,128)} %fusion.159, bf16[3072,2,64]{0,2,1:T(8,128)(2,1)S(1)} %copy-done.6, s32[]{:T(128)S(6)} %min.12, f32[2,512,1536]{2,1,0:T(8,128)} %get-tuple-element.374, ...), kind=kOutput, calls=%fused_computation.27.clone.1 | convolution fusion | flops 212404736 | bytes 25698312 | tf_op jit(solution)/shard_map/while/body/eval_jaxpr/hqk,khd->qhd/dot_general | solution.py:68
  517.4 14.9 %fusion.161 = f32[1536,2,64]{0,2,1:T(8,128)S(1)} fusion(f32[2,512,1536]{2,1,0:T(8,128)} %fusion.159, f32[3072,2,64]{0,2,1:T(8,128)} %get-tuple-element.394, s32[]{:T(128)S(6)} %min.12, bf16[3072,2,64]{0,2,1:T(8,128)(2,1)} %get-tuple-element.414, s32[]{:T(128)S(6)} %select_n.55, f32[2,512,1536]{2,1,0:T(8,128)} %get-tuple-element.374, ...), kind=kOutput, calls=%fused_computation.17.clone.1 | convolution fusion | flops 212535808 | bytes 26877960 | tf_op jit(solution)/shard_map/while/body/eval_jaxpr/hqk,qhd->khd/dot_general | solution.py:71
  562.1 14.9 %fusion.160 = bf16[3072,2,64]{0,2,1:T(8,128)(2,1)} fusion(bf16[3072,2,64]{0,2,1:T(8,128)(2,1)} %get-tuple-element.393, s32[]{:T(128)S(6)} %select_n.55, f32[2,512,1536]{2,1,0:T(8,128)} %fusion.159, bf16[3072,2,64]{0,2,1:T(8,128)(2,1)S(1)} %copy-done.6, s32[]{:T(128)S(6)} %min.12, f32[2,512,1536]{2,1,0:T(8,128)} %get-tuple-element.374, ...), kind=kOutput, calls=%fused_computation.27.clone.1 | convolution fusion | flops 212404736 | bytes 25698312 | tf_op jit(solution)/shard_map/while/body/eval_jaxpr/hqk,khd->qhd/dot_general | solution.py:68
  577.0 15.0 %fusion.161 = f32[1536,2,64]{0,2,1:T(8,128)S(1)} fusion(f32[2,512,1536]{2,1,0:T(8,128)} %fusion.159, f32[3072,2,64]{0,2,1:T(8,128)} %get-tuple-element.394, s32[]{:T(128)S(6)} %min.12, bf16[3072,2,64]{0,2,1:T(8,128)(2,1)} %get-tuple-element.414, s32[]{:T(128)S(6)} %select_n.55, f32[2,512,1536]{2,1,0:T(8,128)} %get-tuple-element.374, ...), kind=kOutput, calls=%fused_computation.17.clone.1 | convolution fusion | flops 212535808 | bytes 26877960 | tf_op jit(solution)/shard_map/while/body/eval_jaxpr/hqk,qhd->khd/dot_general | solution.py:71
  615.6 40.9 %all_to_all.68 = bf16[3072,3,1,128]{3,1,2,0:T(4,128)(2,1)S(1)} all-to-all(bf16[3072,3,1,128]{3,1,2,0:T(4,128)(2,1)S(1)} %copy.83), channel_id=1, replica_groups=mesh['fsdp'=16,'seq'=8] {'seq'}, dimensions={0} | all-to-all | bytes 4718592 | tf_op jit(solution)/shard_map/all_to_all | solution.py:132
  659.4 9.5 %convolution_convert_fusion = bf16[1536,3072]{1,0:T(8,128)(2,1)} fusion(bf16[384,3072]{0,1:T(8,128)(2,1)} %bitcast.106, bf16[1,384,1536]{2,1,0:T(8,128)(2,1)S(1)} %copy-done.1, f32[384]{0:T(512)S(1)} %copy-done.10, f32[384]{0:T(512)S(1)} %copy-done.8), kind=kOutput, calls=%fused_computation.54 | convolution fusion | flops 3630956544 | bytes 12979200 | tf_op jit(solution)/shard_map/dot_general | solution.py:146
  671.8 15.6 %all_to_all.69 = bf16[8,2,24576]{2,1,0:T(2,128)(2,1)S(1)} all-to-all(bf16[8,2,24576]{2,1,0:T(2,128)(2,1)S(1)} %reshape.147), channel_id=1, replica_groups=mesh['fsdp'=16,'seq'=8] {'seq'}, dimensions={0} | all-to-all | bytes 1572864 | tf_op jit(solution)/shard_map/all_to_all | solution.py:131
  689.9 71.7 %reduce-scatter.5.cloned.1.call-done = bf16[96,3072]{1,0:T(8,128)(2,1)} async-done(((bf16[1536,3072]{1,0:T(8,128)(2,1)}), bf16[96,3072]{1,0:T(8,128)(2,1)}) %reduce-scatter.5.cloned.1.call-update) | async-done | bytes 589840 | tf_op jit(solution)/shard_map/reduce_scatter | solution.py:145
  763.8 7.7 fusion.108
  773.2 21.7 %reduce-scatter.7.cloned.1.call-done = bf16[384,96]{1,0:T(8,128)(2,1)} async-done(((bf16[3072,96]{1,0:T(8,128)(2,1)}), bf16[384,96]{1,0:T(8,128)(2,1)}) %reduce-scatter.7.cloned.1.call-update) | async-done | bytes 73744
  (134 shorter events, 231.8 us)
Async XLA Ops:
  13.1 8.4 %copy-start.5 = (bf16[1,384,1024]{2,1,0:T(8,128)(2,1)S(1)}, bf16[1,384,1024]{2,1,0:T(8,128)(2,1)}, u32[]{:S(2)}) copy-start(bf16[1,384,1024]{2,1,0:T(8,128)(2,1)} %param.9) | copy-start | bytes 2359300
  13.1 9.5 %copy-start = (bf16[1,384,1536]{2,1,0:T(8,128)(2,1)S(1)}, bf16[1,384,1536]{2,1,0:T(8,128)(2,1)}, u32[]{:S(2)}) copy-start(bf16[1,384,1536]{2,1,0:T(8,128)(2,1)} %param.6) | copy-start | bytes 3538948
  13.1 173.0 %all-to-all-start = ((bf16[16,96,3072]{2,1,0:T(8,128)(2,1)}), bf16[16,96,3072]{2,1,0:T(8,128)(2,1)}, u32[]{:S(2)}, u32[]{:S(2)}) async-start(bf16[16,96,3072]{2,1,0:T(8,128)(2,1)} %stack.10), calls=%async_computation | async-start | bytes 18874368 | tf_op jit(solution)/shard_map/all_to_all | solution.py:13
  22.8 175.5 %copy-start.7 = (f32[384]{0:T(512)}, f32[384]{0:T(512)S(1)}, u32[]{:S(2)}) copy-start(f32[384]{0:T(512)S(1)} %broadcast_multiply_fusion.2) | copy-start | bytes 4612
  23.3 175.0 %copy-start.9 = (f32[384]{0:T(512)}, f32[384]{0:T(512)S(1)}, u32[]{:S(2)}) copy-start(f32[384]{0:T(512)S(1)} %add_rsqrt_fusion) | copy-start | bytes 4612
  186.1 17.4 %all-to-all-start.2 = ((bf16[384,1,8,128]{0,3,1,2:T(8,128)(2,1)}), bf16[384,1,8,128]{0,3,1,2:T(8,128)(2,1)S(1)}, u32[]{:S(2)}, u32[]{:S(2)}) async-start(bf16[384,1,8,128]{0,3,1,2:T(8,128)(2,1)} %bitcast.17), calls=%async_computation.2 | async-start | bytes 1572864 | tf_op jit(solution)/shard_map/all_to_all | solution.py:118
  200.9 6.4 copy-start.11
  203.5 33.5 %all-to-all-start.1 = ((bf16[384,3,8,128]{3,0,1,2:T(8,128)(2,1)}), bf16[384,3,8,128]{3,0,1,2:T(8,128)(2,1)S(1)}, u32[]{:S(2)}, u32[]{:S(2)}) async-start(bf16[384,3,8,128]{3,0,1,2:T(8,128)(2,1)} %copy.74), calls=%async_computation.1 | async-start | bytes 4718592 | tf_op jit(solution)/shard_map/all_to_all | solution.py:117
  207.2 554.4 %reduce-scatter.5.cloned.1.call-start = ((), (), s32[]{:S(2)}) async-start(), calls=%async_computation.7 | async-start | bytes 10027008 | tf_op jit(solution)/shard_map/reduce_scatter | solution.py:145
  244.5 6.2 copy-start.6
  305.4 6.2 copy-start.6
  366.3 6.2 copy-start.6
  427.0 6.2 copy-start.6
  487.6 6.2 copy-start.6
  547.2 6.2 copy-start.6
  606.2 2.3 copy-start.3
  606.2 2.2 copy-start.2
  656.9 2.5 copy-start.1
  656.9 2.5 copy-start.8
  656.9 2.5 copy-start.10
  668.9 1.1 copy-start.4
  669.0 125.9 %reduce-scatter.7.cloned.1.call-start = ((), (), s32[]{:S(2)}) async-start(), calls=%async_computation.8 | async-start | bytes 884736
Sparse Core Ops, SparseCore 0:
  669.1 92.4 reduce-scatter.4
  764.0 30.8 reduce-scatter.6
